TPU v7x, 32 devices: a whole 2x2x4 slice. The times are simulated.
32 devices in a mesh: groups: 2 (over x), tile: 16 (over z, y, core).
Axes of the slice: x: 2, y: 2, z: 4, core: 2. Of those that a mesh axis runs over, the one named last changes fastest.
Arguments:
- tiles: float32 [2, 12288, 384], P(None, ('groups', 'tile')), parts along dimension 1, may hold values from -6 to 6
- library: float32 [128, 2, 128, 128], P('tile'), may hold values from -6 to 6
- block_owner: int32 [2], replicated, may hold values from 0 to 15
- block_clips: int32 [2, 2], replicated, may hold values from 0 to 7
- layer_order: int32 [32, 2], P(('groups', 'tile')), parts along dimension 0, may hold values from 0 to 1, each once within a row
Outputs:
- scores: float32 [2, 2, 12288, 384], P(None, None, ('groups', 'tile')), parts along dimension 2
- peak_scores: float32 [4, 2], P('groups'), parts along dimension 0
There are 2 independent parts, one for each index of `groups`. A program takes and returns all parts, laid end to end along the dimension named above; an argument that names none is the same for every part. Nothing has to cross between parts.
Inputs may be any that keep to these rules, and one draw needn't show every extreme that they name: `layer_order`: each row is a permutation of 0 to 1.
All inputs are finite; a program needn't handle non-finite values.
Results may differ from a plain program's by a relative error of at most 0.000098.
Values sent between devices are 32-bit elements; how exact they have to be, the bound alone decides.
A program may use at most 128 MiB of HBM per device.

v0:
```python
import functools
import math

import jax
import jax.numpy as jnp
import numpy as np
from jax import lax
from jax.experimental import pallas as pl
from jax.experimental.pallas import tpu as pltpu
from jax.sharding import PartitionSpec as P

F32 = jnp.float32
BF16 = jnp.bfloat16


def split(x):
    high = x.astype(BF16)
    return high, (x - high.astype(F32)).astype(BF16)


def mm(a, b):
    return jnp.dot(a, b, preferred_element_type=F32)


def transform_matrix(extent):
    span = 2 * extent
    odd = 2 * np.arange(extent)[:, None] + 1
    angle = (odd * np.arange(span)[None, :] % (2 * span)) * (math.pi / span)
    return np.concatenate([np.cos(angle), np.sin(angle)], axis=0).astype(np.float32)


def halves(matrix):
    high = matrix.astype(BF16)
    low = (matrix - high.astype(np.float32)).astype(BF16)
    return high, low


def constants(extent):
    forward = transform_matrix(extent)
    fh, fl = halves(forward)
    row_left = np.concatenate([fh, fl, fh], axis=1)
    ft = np.ascontiguousarray(forward.T)
    th, tl = halves(ft)
    col_right = np.stack([th, tl])
    back = forward[:, :extent] * np.float32(1.0 / extent)
    bh, bl = halves(back)
    back_right = np.stack([bh, bl])
    back_left = np.concatenate([bh.T, bl.T, bh.T], axis=1)
    offset = np.arange(2 * extent)[None, :] - np.arange(extent)[:, None]
    band = ((offset >= 0) & (offset < extent)).astype(BF16)
    band_left = np.concatenate([band, band], axis=1)
    band_right = np.ascontiguousarray(band.T)
    return [jnp.asarray(c) for c in (row_left, col_right, back_left, back_right, band_left, band_right)]


def combine(y, e):
    a, b = y[:e, :e], y[:e, e:]
    c, d = y[e:, :e], y[e:, e:]
    return a - d, b + c, a + d, c - b


class Transforms:
    def __init__(self, refs, shapes):
        self.__dict__.update(refs)
        self.layers, self.rows, self.cols, self.e, self.per_block, self.count = shapes
        self.span = 2 * self.e
        self.nc = self.cols // self.e
        self.entries = self.layers * self.e * self.e

    def rows_of(self, b, window):
        e, squares = self.e, None
        for l in range(self.layers):
            x = window(l)
            squares = x * x if squares is None else squares + x * x
            xh, xl = split(x)
            y = mm(self.row_left[...], jnp.concatenate([xh, xh, xl], axis=0))
            h, low = split(y)
            self.yh[l], self.yl[l] = h, low
        sh, sl = split(squares)
        energy = mm(self.band_left[...], jnp.concatenate([sh, sl], axis=0))
        eh, el = split(energy)
        for c in range(self.nc):
            width = min(2, self.nc - c) * e
            at = slice(c * e, c * e + width)
            total = mm(eh[:, at], self.band_right[:width]) + mm(el[:, at], self.band_right[:width])
            self.inv[b, :, c * e:(c + 1) * e] = 1.0 / jnp.sqrt(total / self.entries + 1e-05)

    def columns_of(self, b):
        e = self.e
        for c in range(self.nc):
            width = min(2, self.nc - c) * e
            at = slice(c * e, c * e + width)
            for l in range(self.layers):
                h, low = self.yh[l, :, at], self.yl[l, :, at]
                y = mm(h, self.col_right[0, :width]) + mm(low, self.col_right[0, :width]) + mm(h, self.col_right[1, :width])
                for n, part in enumerate(combine(y, e)):
                    self.tile_parts[b, c, l, n] = part

    def clip_of(self, k, layer_at):
        e, span, row_left, col_right = self.e, self.span, self.row_left, self.col_right
        total = jnp.zeros((e, e), F32)
        for l in range(self.layers):
            chosen = layer_at(l)
            total = total + chosen * chosen
            ch, cl = split(chosen)
            first = mm(row_left[:, :e], ch) + mm(row_left[:, span:span + e], ch) + mm(row_left[:, :e], cl)
            fh, fl = split(first)
            second = mm(fh, col_right[0, :e]) + mm(fl, col_right[0, :e]) + mm(fh, col_right[1, :e])
            for n, part in enumerate(combine(second, e)):
                self.spectra[k, l, n] = part
        mean = jnp.sum(total, keepdims=True) / self.entries
        return 1.0 / (math.sqrt(self.entries) * jnp.sqrt(mean + 1e-05))

    def inverse_of(self, b, clip_scale):
        e = self.e
        for c in range(self.nc):
            for k in range(self.count):
                u1 = u2 = v1 = v2 = None
                for l in range(self.layers):
                    p1, p2, q1, q2 = (self.tile_parts[b, c, l, n] for n in range(4))
                    c1, c2, d1, d2 = (self.spectra[k, l, n] for n in range(4))
                    t = (p1 * c1 + p2 * c2, p2 * c1 - p1 * c2, q1 * d1 + q2 * d2, q2 * d1 - q1 * d2)
                    if u1 is None:
                        u1, u2, v1, v2 = t
                    else:
                        u1, u2, v1, v2 = u1 + t[0], u2 + t[1], v1 + t[2], v2 + t[3]
                z = jnp.concatenate([
                    jnp.concatenate([u1 + v1, u2 - v2], axis=1),
                    jnp.concatenate([u2 + v2, v1 - u1], axis=1)], axis=0)
                zh, zl = split(z)
                w = mm(zh, self.back_right[0]) + mm(zl, self.back_right[0]) + mm(zh, self.back_right[1])
                h, low = split(w)
                self.wh[k, :, c * e:(c + 1) * e] = h
                self.wl[k, :, c * e:(c + 1) * e] = low
        scale = self.inv[b]
        for k in range(self.count):
            out = mm(self.back_left[...], jnp.concatenate([self.wh[k], self.wh[k], self.wl[k]], axis=0))
            out = out * scale * (clip_scale[k] * 0.5)
            self.scores[k // self.per_block, k % self.per_block, pl.ds(pl.multiple_of(b * e, e), e)] = out
            top = jnp.max(out, axis=0, keepdims=True)
            best = self.peaks[k:k + 1]
            for c in range(self.nc):
                best = jnp.maximum(best, top[:, c * e:(c + 1) * e])
            self.peaks[k:k + 1] = best


MESH = pl.DeviceIdType.MESH
PLANE = 4
CHUNKS = 4


def kernel(tiles_n, owner, picks, order, *refs):
    sources = refs[:8]
    (scores, peak_out,
           yh, yl, inv, tile_parts, spectra, wh, wl, peaks, slots,
           stage, landed, mine, rbuf, lbuf, rsend, lsend, full, halo_in,
           rs_send, rs_recv, r_send, r_recv, l_send, l_recv,
           ag_send, ag_recv, fw_send, fw_recv, halo_send, halo_recv, peak_send, peak_recv,
           library, tiles, row_left, col_right, back_left, back_right, band_left, band_right, load_sem) = refs[8:]
    loads = [pltpu.make_async_copy(a, b, load_sem.at[n]) for n, (a, b) in enumerate(zip(
        sources, (library, tiles, row_left, col_right, back_left, back_right, band_left, band_right)))]
    for load in loads:
        load.start()
    g = lax.axis_index("groups")
    t = lax.axis_index("tile")
    per_block = picks.shape[1]
    layers, rows, cols = tiles.shape
    e = library.shape[-1]
    nr = rows // e
    count = picks.shape[0] * per_block
    work = Transforms(dict(row_left=row_left, col_right=col_right, back_left=back_left, back_right=back_right,
                           band_left=band_left, band_right=band_right, scores=scores, yh=yh, yl=yl, inv=inv,
                           tile_parts=tile_parts, spectra=spectra, wh=wh, wl=wl, peaks=peaks),
                      (layers, rows, cols, e, per_block, count))
    z = t // PLANE
    q = lax.rem(t, PLANE)
    depth = tiles_n // PLANE
    parity = lax.rem(g, 2)
    other_g = g + 1 - 2 * parity
    core = lax.rem(q, 2)
    partner = t + 1 - 2 * core
    upper = q // 2
    across = t + 2 - 4 * upper
    plane = [z * PLANE + lax.rem(q + d, PLANE) for d in range(1, PLANE)]
    others = [(g, lax.rem(t + d, tiles_n)) for d in range(1, tiles_n)]
    greeted = others + [(other_g, t), (other_g, across)]

    barrier = pltpu.get_barrier_semaphore()
    for target in greeted:
        pl.semaphore_signal(barrier, inc=1, device_id=target, device_id_type=MESH)

    loads[0].wait()

    def contribution(slab):
        clip, layer = slab // layers, lax.rem(slab, layers)
        block, which = clip // per_block, lax.rem(clip, per_block)
        mask = jnp.where(owner[block] == t, 1.0, 0.0).astype(F32)
        return library[picks[block, which], layer] * mask

    for d in range(PLANE):
        stage[d] = contribution(parity * PLANE + lax.rem(q + d, PLANE))

    @pl.when(z == 0)
    def _():
        rbuf[...] = jnp.zeros_like(rbuf)

    @pl.when(z == depth - 1)
    def _():
        lbuf[...] = jnp.zeros_like(lbuf)

    @pl.when(t == tiles_n - 1)
    def _():
        halo_in[...] = jnp.zeros_like(halo_in)

    peaks[...] = jnp.full(peaks.shape, -jnp.inf, F32)
    pl.semaphore_wait(barrier, len(greeted))

    def remote(src, dst, send, recv, target):
        return pltpu.make_async_remote_copy(src_ref=src, dst_ref=dst, send_sem=send, recv_sem=recv,
                                            device_id=target, device_id_type=MESH)

    scatter = []
    for d in range(1, PLANE):
        copy = remote(stage.at[d], landed.at[d - 1], rs_send.at[d - 1], rs_recv.at[d - 1], (g, plane[d - 1]))
        copy.start()
        scatter.append(copy)
    for load in loads[1:]:
        load.wait()
    work.rows_of(0, lambda l: tiles[l, :2 * e])
    for copy in scatter:
        copy.wait()
    mine[...] = stage[0] + landed[0] + landed[1] + landed[2]

    step = e // CHUNKS
    parts = [pl.ds(c * step, step) for c in range(CHUNKS)]
    slab = parity * PLANE + q
    right = [remote(rsend.at[c], rbuf.at[c], r_send.at[c], r_recv.at[c], (g, t + PLANE)) for c in range(CHUNKS)]
    left = [remote(lsend.at[c], lbuf.at[c], l_send.at[c], l_recv.at[c], (g, t - PLANE)) for c in range(CHUNKS)]
    forwards = []
    slabs = [slab, (1 - parity) * PLANE + q,
             parity * PLANE + q + 2 - 4 * upper, (1 - parity) * PLANE + q + 2 - 4 * upper]
    targets = [(other_g, t), (g, across), (other_g, across)]

    def forward(n, c):
        copy = remote(full.at[slabs[n], parts[c]], full.at[slabs[n], parts[c]],
                      fw_send.at[n, c], fw_recv.at[n, c], (g, partner))
        copy.start()
        forwards.append(copy)

    gathers = [(n, c, remote(full.at[slab, parts[c]], full.at[slab, parts[c]], ag_send.at[n, c], ag_recv.at[n, c], target))
               for c in range(CHUNKS) for n, target in enumerate(targets)]
    own = [remote(full.at[slab, parts[c]], full.at[slab, parts[c]], fw_send.at[0, c], fw_recv.at[0, c], (g, partner))
           for c in range(CHUNKS)]

    def rightward(c):
        @pl.when(z > 0)
        def _():
            right[c].wait_recv()
        rsend[c] = rbuf[c] + mine[parts[c]]

        @pl.when(z < depth - 1)
        def _():
            right[c].start()

    def leftward(c):
        @pl.when(z < depth - 1)
        def _():
            left[c].wait_recv()
        lsend[c] = lbuf[c] + mine[parts[c]]

        @pl.when(z > 0)
        def _():
            left[c].start()

    def deliver(c):
        full[slab, parts[c]] = rsend[c] + lbuf[c]
        for n in range(3):
            gathers[3 * c + n][2].start()
        own[c].start()

    lower = z < depth // 2
    for condition, first, second in ((lower, rightward, leftward), (jnp.logical_not(lower), leftward, rightward)):
        @pl.when(condition)
        def _(first=first, second=second):
            for c in range(CHUNKS):
                first(c)
            for c in range(CHUNKS):
                second(c)
                deliver(c)
    forwards.extend(own)
    work.columns_of(0)
    work.rows_of(1, lambda l: tiles[l, e:3 * e])
    for n, c, copy in gathers:
        copy.wait_recv()
        forward(n + 1, c)
    halo = remote(tiles.at[:, pl.ds(0, e)], halo_in, halo_send, halo_recv, (g, t - 1))

    @pl.when(t > 0)
    def _():
        halo.start()

    for b in range(1, nr - 1):
        if b > 1:
            work.rows_of(b, lambda l: tiles[l, b * e:(b + 2) * e])
        work.columns_of(b)
    for copy in forwards:
        copy.wait_recv()
    clip_scale = [work.clip_of(k, lambda l: full[k * layers + order[0, l]]) for k in range(count)]

    def row_block(b, carry):
        @pl.when(b == nr - 1)
        def _():
            @pl.when(t < tiles_n - 1)
            def _():
                halo.wait_recv()
            work.rows_of(nr - 1, lambda l: jnp.concatenate([tiles[l, rows - e:], halo_in[l]], axis=0))
            work.columns_of(nr - 1)
        work.inverse_of(b, clip_scale)
        return carry

    lax.fori_loop(0, nr, row_block, 0)

    copies = [remote(peaks, slots.at[n], peak_send.at[n], peak_recv.at[n], target) for n, target in enumerate(others)]
    for copy in copies:
        copy.start()
    for _, _, copy in gathers:
        copy.wait_send()
    for copy in forwards:
        copy.wait_send()
    for c in range(CHUNKS):
        @pl.when(z < depth - 1)
        def _(c=c):
            right[c].wait_send()

        @pl.when(z > 0)
        def _(c=c):
            left[c].wait_send()

    @pl.when(t > 0)
    def _():
        halo.wait_send()

    best = peaks[...]
    for n, copy in enumerate(copies):
        copy.wait_recv()
        best = jnp.maximum(best, slots[n])
    best = jnp.max(best, axis=1, keepdims=True)
    for k in range(count):
        at = k % per_block
        peak_out[k // per_block:k // per_block + 1, at:at + 1] = best[k:k + 1]
    for copy in copies:
        copy.wait_send()


def local(tiles, library, block_owner, block_clips, layer_order):
    layers, rows, cols = tiles.shape
    e = library.shape[-1]
    span, nr, nc = 2 * e, rows // e, cols // e
    blocks, per_block = block_clips.shape
    count = blocks * per_block
    slabs = count * layers
    assert slabs == 2 * PLANE
    tiles_n = lax.axis_size("tile")
    smem = pl.BlockSpec(memory_space=pltpu.SMEM)
    vmem = pl.BlockSpec(memory_space=pltpu.VMEM)
    dma = pltpu.SemaphoreType.DMA
    piece = pltpu.VMEM((CHUNKS, e // CHUNKS, e), F32)
    lines = -(-count // 8) * 8
    operands = [library, tiles, *constants(e)]
    return pl.pallas_call(
        functools.partial(kernel, tiles_n),
        out_shape=(jax.ShapeDtypeStruct((blocks, per_block, rows, cols), F32),
                   jax.ShapeDtypeStruct((blocks, per_block), F32)),
        in_specs=[smem] * 3 + [pl.BlockSpec(memory_space=pltpu.HBM)] * 8,
        out_specs=(vmem, vmem),
        scratch_shapes=[
            pltpu.VMEM((layers, span, cols), BF16), pltpu.VMEM((layers, span, cols), BF16),
            pltpu.VMEM((nr, e, cols), F32),
            pltpu.VMEM((nr, nc, layers, 4, e, e), F32), pltpu.VMEM((count, layers, 4, e, e), F32),
            pltpu.VMEM((count, span, cols), BF16), pltpu.VMEM((count, span, cols), BF16),
            pltpu.VMEM((lines, e), F32), pltpu.VMEM((tiles_n - 1, lines, e), F32),
            pltpu.VMEM((PLANE, e, e), F32), pltpu.VMEM((PLANE - 1, e, e), F32), pltpu.VMEM((e, e), F32),
            piece, piece, piece, piece,
            pltpu.VMEM((slabs, e, e), F32), pltpu.VMEM((layers, e, cols), F32),
            dma((PLANE - 1,)), dma((PLANE - 1,)), dma((CHUNKS,)), dma((CHUNKS,)), dma((CHUNKS,)), dma((CHUNKS,)),
            dma((3, CHUNKS)), dma((3, CHUNKS)), dma((4, CHUNKS)), dma((4, CHUNKS)), dma, dma,
            dma((tiles_n - 1,)), dma((tiles_n - 1,)),
        ] + [pltpu.VMEM(a.shape, a.dtype) for a in operands] + [dma((len(operands),))],
        compiler_params=pltpu.CompilerParams(collective_id=0, has_side_effects=True, vmem_limit_bytes=60 * 1024 * 1024),
    )(block_owner, block_clips, layer_order, *operands)


def solution(mesh):
    in_specs = (
        P(None, ("groups", "tile"), None),
        P("tile", None, None, None),
        P(),
        P(),
        P(("groups", "tile"), None),
    )
    out_specs = (P(None, None, ("groups", "tile"), None), P("groups", None))
    return jax.shard_map(local, mesh=mesh, in_specs=in_specs, out_specs=out_specs, check_vma=False)
```

profile of v0, /device:TPU:0, one launch (start us, length us, event | category | flops | bytes accessed | tf_op | source)
XLA Modules:
  0.0 46.3 jit_solution(10190116596824339276)
XLA Ops:
  0.6 41.9 %shard_map.122 = (f32[2,2,384,384]{3,2,1,0:T(8,128)}, f32[2,2]{1,0:T(2,128)}) custom-call(s32[2]{0:T(128)} %owner.1, s32[2,2]{1,0:T(2,128)} %picks.1, s32[1,2]{1,0:T(1,128)} %order.1, f32[8,2,128,128]{3,2,1,0:T(8,128)} %refs_0_.1, f32[2,384,384]{2,1,0:T(8,128)} %refs_1_.1, bf16[256,768]{1,0:T(8,128)(2,1)} %constant.12.clone.refs_2_, ...), custom_call_target="tpu_custom_call" | custom-call | tf_op jit(solution)/shard_map/pallas_call | solution.py:370
  42.5 0.0 copy-start
  42.5 3.2 %copy.15 = f32[2,2,384,384]{3,2,1,0:T(8,128)} copy(f32[2,2,384,384]{3,2,1,0:T(8,128)} %get-tuple-element.4) | data formatting | bytes 4718592
  45.7 0.0 copy-done
  45.7 0.6 %copy.16 = f32[2,2]{1,0:T(2,128)} copy(f32[2,2]{1,0:T(2,128)S(1)} %copy-done) | data formatting | bytes 32
Async XLA Ops:
  42.5 3.2 %copy-start = (f32[2,2]{1,0:T(2,128)S(1)}, f32[2,2]{1,0:T(2,128)}, u32[]{:S(2)}) copy-start(f32[2,2]{1,0:T(2,128)} %get-tuple-element.5) | copy-start | bytes 52
where the time goes:
time: 46.5 us; the launch traced here: 46.3 us
  Pallas kernels  41.9 us (90%)
  local copies, waits for them, and re-layouts  3.79 us (8%)
  between operations  0.65 us (1%)
    pallas_call x1, Pallas kernels, local(): pl.pallas_call(functools.partial(kernel, tiles_n), out_shape=(jax.ShapeDt...  41.9 us
    unnamed x4, local copies, waits for them, and re-layouts  3.79 us

commit v1 on v0

--- a/solution.py
+++ b/solution.py
@@ -352,6 +352,14 @@
         copy.wait_send()
 
 
+def write_out(scores, peaks, scores_out, peaks_out, sem):
+    copies = [pltpu.make_async_copy(scores, scores_out, sem.at[0]), pltpu.make_async_copy(peaks, peaks_out, sem.at[1])]
+    for copy in copies:
+        copy.start()
+    for copy in copies:
+        copy.wait()
+
+
 def local(tiles, library, block_owner, block_clips, layer_order):
     layers, rows, cols = tiles.shape
     e = library.shape[-1]
@@ -367,10 +375,10 @@
     piece = pltpu.VMEM((CHUNKS, e // CHUNKS, e), F32)
     lines = -(-count // 8) * 8
     operands = [library, tiles, *constants(e)]
-    return pl.pallas_call(
+    scores, peaks = pl.pallas_call(
         functools.partial(kernel, tiles_n),
-        out_shape=(jax.ShapeDtypeStruct((blocks, per_block, rows, cols), F32),
-                   jax.ShapeDtypeStruct((blocks, per_block), F32)),
+        out_shape=(pltpu.VMEM((blocks, per_block, rows, cols), F32),
+                   pltpu.VMEM((blocks, per_block), F32)),
         in_specs=[smem] * 3 + [pl.BlockSpec(memory_space=pltpu.HBM)] * 8,
         out_specs=(vmem, vmem),
         scratch_shapes=[
@@ -386,8 +394,18 @@
             dma((3, CHUNKS)), dma((3, CHUNKS)), dma((4, CHUNKS)), dma((4, CHUNKS)), dma, dma,
             dma((tiles_n - 1,)), dma((tiles_n - 1,)),
         ] + [pltpu.VMEM(a.shape, a.dtype) for a in operands] + [dma((len(operands),))],
-        compiler_params=pltpu.CompilerParams(collective_id=0, has_side_effects=True, vmem_limit_bytes=60 * 1024 * 1024),
+        compiler_params=pltpu.CompilerParams(collective_id=0, has_side_effects=True, vmem_limit_bytes=64600000),
     )(block_owner, block_clips, layer_order, *operands)
+    hbm = pl.BlockSpec(memory_space=pltpu.HBM)
+    scores, peaks = (pltpu.with_memory_space_constraint(a, pltpu.VMEM) for a in (scores, peaks))
+    return pl.pallas_call(
+        write_out,
+        out_shape=(jax.ShapeDtypeStruct(scores.shape, F32), jax.ShapeDtypeStruct(peaks.shape, F32)),
+        in_specs=[vmem, vmem],
+        out_specs=(hbm, hbm),
+        scratch_shapes=[dma((2,))],
+        compiler_params=pltpu.CompilerParams(vmem_limit_bytes=1024 * 1024),
+    )(scores, peaks)
 
 
 def solution(mesh):

time: 46.5 us -> 42.6 us (0.916)
  local copies, waits for them, and re-layouts: 3.79 us -> 0 us
    unnamed x4 -> x0, local copies, waits for them, and re-layouts: 3.79 us -> none
    pallas_call x1 -> x2, Pallas kernels: 41.9 us -> 41.8 us  [the longest x1 40.4 us: local(): pl.pallas_call(functools.partial(kernel, tiles_n), out_shape=(pltpu.VMEM(...]
where the time goes in v1:
time: 42.6 us; the launch traced here: 42.4 us
  Pallas kernels  41.8 us (98%)
  between operations  0.64 us (2%)
    pallas_call x1, Pallas kernels, local(): pl.pallas_call(functools.partial(kernel, tiles_n), out_shape=(pltpu.VMEM(...  40.4 us
    pallas_call x1, Pallas kernels, local(): pl.pallas_call(write_out, out_shape=(jax.ShapeDtypeStruct(scores.shape, F...  1.43 us

profile of v1, /device:TPU:0, one launch (start us, length us, event | category | flops | bytes accessed | tf_op | source)
XLA Modules:
  0.0 42.4 jit_solution(13513364898088249022)
XLA Ops:
  0.6 40.4 %shard_map.122 = (f32[2,2,384,384]{3,2,1,0:T(8,128)S(1)}, f32[2,2]{1,0:T(2,128)S(1)}) custom-call(s32[2]{0:T(128)} %owner.1, s32[2,2]{1,0:T(2,128)} %picks.1, s32[1,2]{1,0:T(1,128)} %order.1, f32[8,2,128,128]{3,2,1,0:T(8,128)} %refs_0_.1, f32[2,384,384]{2,1,0:T(8,128)} %refs_1_.1, bf16[256,768]{1,0:T(8,128)(2,1)} %constant.12.clone.refs_2_, ...), custom_call_target="tpu_custom_call" | custom-call | tf_op jit(solution)/shard_map/pallas_call | solution.py:378
  41.0 1.4 %shard_map.123 = (f32[2,2,384,384]{3,2,1,0:T(8,128)}, f32[2,2]{1,0:T(2,128)}) custom-call(f32[2,2,384,384]{3,2,1,0:T(8,128)S(1)} %get-tuple-element.4.scores, f32[2,2]{1,0:T(2,128)S(1)} %get-tuple-element.5.peaks), custom_call_target="tpu_custom_call" | custom-call | tf_op jit(solution)/shard_map/pallas_call | solution.py:401

commit v2 on v1

v2 whole, which is shorter than its diff:
```python
import functools
import math

import jax
import jax.numpy as jnp
import numpy as np
from jax import lax
from jax.experimental import pallas as pl
from jax.experimental.pallas import tpu as pltpu
from jax.sharding import PartitionSpec as P

F32 = jnp.float32
BF16 = jnp.bfloat16


def split(x):
    high = x.astype(BF16)
    return high, (x - high.astype(F32)).astype(BF16)


def mm(a, b):
    return jnp.dot(a, b, preferred_element_type=F32)


def transform_matrix(extent):
    span = 2 * extent
    odd = 2 * np.arange(extent)[:, None] + 1
    angle = (odd * np.arange(span)[None, :] % (2 * span)) * (math.pi / span)
    return np.concatenate([np.cos(angle), np.sin(angle)], axis=0).astype(np.float32)


def halves(matrix):
    high = matrix.astype(BF16)
    low = (matrix - high.astype(np.float32)).astype(BF16)
    return high, low


def constants(extent):
    forward = transform_matrix(extent)
    fh, fl = halves(forward)
    row_left = np.concatenate([fh, fl, fh], axis=1)
    ft = np.ascontiguousarray(forward.T)
    th, tl = halves(ft)
    col_right = np.stack([th, tl])
    back = forward[:, :extent] * np.float32(1.0 / extent)
    bh, bl = halves(back)
    back_right = np.stack([bh, bl])
    back_left = np.concatenate([bh.T, bl.T, bh.T], axis=1)
    offset = np.arange(2 * extent)[None, :] - np.arange(extent)[:, None]
    band = ((offset >= 0) & (offset < extent)).astype(BF16)
    band_left = np.concatenate([band, band], axis=1)
    band_right = np.ascontiguousarray(band.T)
    return [jnp.asarray(c) for c in (row_left, col_right, back_left, back_right, band_left, band_right)]


def combine(y, e):
    a, b = y[:e, :e], y[:e, e:]
    c, d = y[e:, :e], y[e:, e:]
    return a - d, b + c, a + d, c - b


class Transforms:
    def __init__(self, refs, shapes):
        self.__dict__.update(refs)
        self.layers, self.rows, self.cols, self.e, self.per_block, self.count = shapes
        self.span = 2 * self.e
        self.nc = self.cols // self.e
        self.entries = self.layers * self.e * self.e

    def rows_of(self, b, window):
        e, squares = self.e, None
        for l in range(self.layers):
            x = window(l)
            squares = x * x if squares is None else squares + x * x
            xh, xl = split(x)
            y = mm(self.row_left[...], jnp.concatenate([xh, xh, xl], axis=0))
            h, low = split(y)
            self.yh[l], self.yl[l] = h, low
        sh, sl = split(squares)
        energy = mm(self.band_left[...], jnp.concatenate([sh, sl], axis=0))
        eh, el = split(energy)
        for c in range(self.nc):
            width = min(2, self.nc - c) * e
            at = slice(c * e, c * e + width)
            total = mm(eh[:, at], self.band_right[:width]) + mm(el[:, at], self.band_right[:width])
            self.inv[b, :, c * e:(c + 1) * e] = 1.0 / jnp.sqrt(total / self.entries + 1e-05)

    def columns_of(self, b):
        e = self.e
        for c in range(self.nc):
            width = min(2, self.nc - c) * e
            at = slice(c * e, c * e + width)
            for l in range(self.layers):
                h, low = self.yh[l, :, at], self.yl[l, :, at]
                y = mm(h, self.col_right[0, :width]) + mm(low, self.col_right[0, :width]) + mm(h, self.col_right[1, :width])
                for n, part in enumerate(combine(y, e)):
                    self.tile_parts[b, c, l, n] = part

    def clip_of(self, k, layer_at):
        e, span, row_left, col_right = self.e, self.span, self.row_left, self.col_right
        total = jnp.zeros((e, e), F32)
        for l in range(self.layers):
            chosen = layer_at(l)
            total = total + chosen * chosen
            ch, cl = split(chosen)
            first = mm(row_left[:, :e], ch) + mm(row_left[:, span:span + e], ch) + mm(row_left[:, :e], cl)
            fh, fl = split(first)
            second = mm(fh, col_right[0, :e]) + mm(fl, col_right[0, :e]) + mm(fh, col_right[1, :e])
            for n, part in enumerate(combine(second, e)):
                self.spectra[k, l, n] = part
        mean = jnp.sum(total, keepdims=True) / self.entries
        return 1.0 / (math.sqrt(self.entries) * jnp.sqrt(mean + 1e-05))

    def inverse_of(self, b, k, clip_scale):
        e = self.e
        for c in range(self.nc):
            u1 = u2 = v1 = v2 = None
            for l in range(self.layers):
                p1, p2, q1, q2 = (self.tile_parts[b, c, l, n] for n in range(4))
                c1, c2, d1, d2 = (self.spectra[k, self.order[0, l], n] for n in range(4))
                t = (p1 * c1 + p2 * c2, p2 * c1 - p1 * c2, q1 * d1 + q2 * d2, q2 * d1 - q1 * d2)
                if u1 is None:
                    u1, u2, v1, v2 = t
                else:
                    u1, u2, v1, v2 = u1 + t[0], u2 + t[1], v1 + t[2], v2 + t[3]
            z = jnp.concatenate([
                jnp.concatenate([u1 + v1, u2 - v2], axis=1),
                jnp.concatenate([u2 + v2, v1 - u1], axis=1)], axis=0)
            zh, zl = split(z)
            w = mm(zh, self.back_right[0]) + mm(zl, self.back_right[0]) + mm(zh, self.back_right[1])
            h, low = split(w)
            self.wh[k, :, c * e:(c + 1) * e] = h
            self.wl[k, :, c * e:(c + 1) * e] = low
        out = mm(self.back_left[...], jnp.concatenate([self.wh[k], self.wh[k], self.wl[k]], axis=0))
        out = out * self.inv[b] * (clip_scale * 0.5)
        self.scores[k // self.per_block, k % self.per_block, pl.ds(pl.multiple_of(b * e, e), e)] = out
        top = jnp.max(out, axis=0, keepdims=True)
        best = self.peaks[k:k + 1]
        for c in range(self.nc):
            best = jnp.maximum(best, top[:, c * e:(c + 1) * e])
        self.peaks[k:k + 1] = best


MESH = pl.DeviceIdType.MESH
PLANE = 4
HUBS = 2 * PLANE
CHUNKS = 4


def kernel(tiles_n, owner, picks, order, *refs):
    sources = refs[:8]
    (scores, peak_out,
           yh, yl, inv, tile_parts, spectra, wh, wl, peaks, slots,
           stage, land, full, halo_in,
           rs_send, rs_recv, ag_send, near_recv, far_recv, pair_send, pair_recv,
           halo_send, halo_recv, peak_send, peak_recv,
           library, tiles, row_left, col_right, back_left, back_right, band_left, band_right, load_sem) = refs[8:]
    loads = [pltpu.make_async_copy(a, b, load_sem.at[n]) for n, (a, b) in enumerate(zip(
        sources, (library, tiles, row_left, col_right, back_left, back_right, band_left, band_right)))]
    for load in loads:
        load.start()
    g = lax.axis_index("groups")
    t = lax.axis_index("tile")
    per_block = picks.shape[1]
    layers, rows, cols = tiles.shape
    e = library.shape[-1]
    nr = rows // e
    count = picks.shape[0] * per_block
    work = Transforms(dict(row_left=row_left, col_right=col_right, back_left=back_left, back_right=back_right,
                           band_left=band_left, band_right=band_right, scores=scores, yh=yh, yl=yl, inv=inv,
                           tile_parts=tile_parts, spectra=spectra, wh=wh, wl=wl, peaks=peaks, order=order),
                      (layers, rows, cols, e, per_block, count))
    parity = lax.rem(g, 2)
    other_g = g + 1 - 2 * parity
    core = lax.rem(t, 2)
    partner = (g, t + 1 - 2 * core)
    first_hub = (tiles_n // PLANE // 2 - 1) * PLANE
    is_hub = jnp.logical_and(t >= first_hub, t < first_hub + HUBS)
    others = [(g, lax.rem(t + d, tiles_n)) for d in range(1, tiles_n)]

    barrier = pltpu.get_barrier_semaphore()

    def greet(target):
        pl.semaphore_signal(barrier, inc=1, device_id=target, device_id_type=MESH)

    @pl.when(is_hub)
    def _():
        for target in others:
            greet(target)

    for n in range(HUBS // 2):
        greet((other_g, first_hub + 2 * n + core))

    lanes = count * layers // 2
    width = lanes // CHUNKS
    part = e // HUBS
    loads[0].wait()
    for j in range(lanes):
        slab = 2 * j + parity
        clip, layer = slab // layers, lax.rem(slab, layers)
        block, which = clip // per_block, lax.rem(clip, per_block)
        mask = jnp.where(owner[block] == t, 1.0, 0.0).astype(F32)
        stage[j] = library[picks[block, which], layer] * mask

    pl.semaphore_wait(barrier, jnp.where(is_hub, HUBS - 1 + tiles_n // 2, HUBS))

    def remote(src, dst, send, recv, target):
        return pltpu.make_async_remote_copy(src_ref=src, dst_ref=dst, send_sem=send, recv_sem=recv,
                                            device_id=target, device_id_type=MESH)

    def place(hub):
        at = lax.rem(hub, 2) * (HUBS // 2) + hub // 2
        return pl.ds(pl.multiple_of(at * part, part), part)

    def lane(m):
        return pl.ds(m * width, width)

    mine = pl.ds(pl.multiple_of(core * (e // 2), e // 2), e // 2)
    for m in range(CHUNKS):
        for n in range(HUBS):
            hub = lax.rem(t + n, HUBS)
            target = first_hub + hub
            slot = lax.rem(t - target + tiles_n, tiles_n) - 1

            @pl.when(t != target)
            def _(m=m, hub=hub, target=target, slot=slot):
                remote(stage.at[lane(m), place(hub)], land.at[slot, lane(m)],
                       rs_send.at[m], rs_recv.at[m], (g, target)).start()

    @pl.when(t == tiles_n - 1)
    def _():
        halo_in[...] = jnp.zeros_like(halo_in)

    peaks[...] = jnp.full(peaks.shape, -jnp.inf, F32)
    for load in loads[1:]:
        load.wait()
    for b in range(nr - 1):
        work.rows_of(b, lambda l: tiles[l, b * e:(b + 2) * e])
        work.columns_of(b)

    @pl.when(is_hub)
    def _():
        at = place(t - first_hub)
        for m in range(CHUNKS):
            remote(land.at[:, lane(m)], land.at[:, lane(m)], rs_send.at[m], rs_recv.at[m], partner).wait_recv()
            total = stage[lane(m), at]
            for d in range(tiles_n - 1):
                total = total + land[d, lane(m)]
            full[parity, lane(m), at] = total
            piece = full.at[parity, lane(m), at]
            for n in range(1, tiles_n // 2):
                remote(piece, piece, ag_send.at[m], near_recv.at[m], (g, lax.rem(t + 2 * n, tiles_n))).start()
            for n in range(tiles_n // 2):
                remote(piece, piece, ag_send.at[m], far_recv.at[m], (other_g, lax.rem(t + 2 * n, tiles_n))).start()

    halo = remote(tiles.at[:, pl.ds(0, e)], halo_in, halo_send, halo_recv, (g, t - 1))
    pairs = [remote(full.at[:, lane(m), mine], full.at[:, lane(m), mine], pair_send.at[m], pair_recv.at[m], partner)
             for m in range(CHUNKS)]

    def arrive(m):
        far = full.at[0, lane(m), mine]
        remote(far, far, ag_send.at[m], far_recv.at[m], partner).wait_recv()

        @pl.when(is_hub)
        def _():
            near = full.at[0, lane(m), pl.ds(0, e // 2 - part)]
            remote(near, near, ag_send.at[m], near_recv.at[m], partner).wait_recv()

        @pl.when(jnp.logical_not(is_hub))
        def _():
            remote(far, far, ag_send.at[m], near_recv.at[m], partner).wait_recv()

        pairs[m].start()

    scale = {}

    def clips_in(m):
        slabs = range(2 * m * width, 2 * (m + 1) * width)
        return [k for k in range(count) if (k + 1) * layers - 1 in slabs]

    def slab_of(k, l):
        return full[(k * layers + l) % 2, (k * layers + l) // 2]

    for m in range(CHUNKS + 1):
        if m < CHUNKS:
            arrive(m)
        if m == 0:
            @pl.when(t > 0)
            def _():
                halo.start()
        else:
            pairs[m - 1].wait_recv()
            for k in clips_in(m - 1):
                scale[k] = work.clip_of(k, lambda l: slab_of(k, l))
                for b in range(nr - 1):
                    work.inverse_of(b, k, scale[k])

    @pl.when(t < tiles_n - 1)
    def _():
        halo.wait_recv()
    work.rows_of(nr - 1, lambda l: jnp.concatenate([tiles[l, rows - e:], halo_in[l]], axis=0))
    work.columns_of(nr - 1)
    for k in range(count):
        work.inverse_of(nr - 1, k, scale[k])

    copies = [remote(peaks, slots.at[n], peak_send, peak_recv, target) for n, target in enumerate(others)]
    for copy in copies:
        copy.start()
    for m in range(CHUNKS):
        pairs[m].wait_send()

        @pl.when(is_hub)
        def _(m=m):
            sent = stage.at[lane(m), pl.ds(0, e - part)]
            remote(sent, sent, rs_send.at[m], rs_recv.at[m], partner).wait_send()
            remote(land.at[:, lane(m)], land.at[:, lane(m)], ag_send.at[m], near_recv.at[m], partner).wait_send()

        @pl.when(jnp.logical_not(is_hub))
        def _(m=m):
            sent = stage.at[lane(m)]
            remote(sent, sent, rs_send.at[m], rs_recv.at[m], partner).wait_send()

    @pl.when(t > 0)
    def _():
        halo.wait_send()

    best = peaks[...]
    remote(slots, slots, peak_send, peak_recv, partner).wait_recv()
    for n in range(tiles_n - 1):
        best = jnp.maximum(best, slots[n])
    best = jnp.max(best, axis=1, keepdims=True)
    for k in range(count):
        at = k % per_block
        peak_out[k // per_block:k // per_block + 1, at:at + 1] = best[k:k + 1]
    remote(slots, slots, peak_send, peak_recv, partner).wait_send()


def write_out(scores, peaks, scores_out, peaks_out, sem):
    copies = [pltpu.make_async_copy(scores, scores_out, sem.at[0]), pltpu.make_async_copy(peaks, peaks_out, sem.at[1])]
    for copy in copies:
        copy.start()
    for copy in copies:
        copy.wait()


def local(tiles, library, block_owner, block_clips, layer_order):
    layers, rows, cols = tiles.shape
    e = library.shape[-1]
    span, nr, nc = 2 * e, rows // e, cols // e
    blocks, per_block = block_clips.shape
    count = blocks * per_block
    slabs = count * layers
    lanes = slabs // 2
    assert slabs % 2 == 0 and lanes % CHUNKS == 0
    tiles_n = lax.axis_size("tile")
    smem = pl.BlockSpec(memory_space=pltpu.SMEM)
    vmem = pl.BlockSpec(memory_space=pltpu.VMEM)
    dma = pltpu.SemaphoreType.DMA
    lines = -(-count // 8) * 8
    operands = [library, tiles, *constants(e)]
    scores, peaks = pl.pallas_call(
        functools.partial(kernel, tiles_n),
        out_shape=(pltpu.VMEM((blocks, per_block, rows, cols), F32),
                   pltpu.VMEM((blocks, per_block), F32)),
        in_specs=[smem] * 3 + [pl.BlockSpec(memory_space=pltpu.HBM)] * 8,
        out_specs=(vmem, vmem),
        scratch_shapes=[
            pltpu.VMEM((layers, span, cols), BF16), pltpu.VMEM((layers, span, cols), BF16),
            pltpu.VMEM((nr, e, cols), F32),
            pltpu.VMEM((nr, nc, layers, 4, e, e), F32), pltpu.VMEM((count, layers, 4, e, e), F32),
            pltpu.VMEM((count, span, cols), BF16), pltpu.VMEM((count, span, cols), BF16),
            pltpu.VMEM((lines, e), F32), pltpu.VMEM((tiles_n - 1, lines, e), F32),
            pltpu.VMEM((lanes, e, e), F32), pltpu.VMEM((tiles_n - 1, lanes, e // HUBS, e), F32),
            pltpu.VMEM((2, lanes, e, e), F32), pltpu.VMEM((layers, e, cols), F32),
            *[dma((CHUNKS,))] * 7, dma, dma, dma, dma,
        ] + [pltpu.VMEM(a.shape, a.dtype) for a in operands] + [dma((len(operands),))],
        compiler_params=pltpu.CompilerParams(collective_id=0, has_side_effects=True, vmem_limit_bytes=64600000),
    )(block_owner, block_clips, layer_order, *operands)
    hbm = pl.BlockSpec(memory_space=pltpu.HBM)
    scores, peaks = (pltpu.with_memory_space_constraint(a, pltpu.VMEM) for a in (scores, peaks))
    return pl.pallas_call(
        write_out,
        out_shape=(jax.ShapeDtypeStruct(scores.shape, F32), jax.ShapeDtypeStruct(peaks.shape, F32)),
        in_specs=[vmem, vmem],
        out_specs=(hbm, hbm),
        scratch_shapes=[dma((2,))],
        compiler_params=pltpu.CompilerParams(vmem_limit_bytes=1024 * 1024),
    )(scores, peaks)


def solution(mesh):
    in_specs = (
        P(None, ("groups", "tile"), None),
        P("tile", None, None, None),
        P(),
        P(),
        P(("groups", "tile"), None),
    )
    out_specs = (P(None, None, ("groups", "tile"), None), P("groups", None))
    return jax.shard_map(local, mesh=mesh, in_specs=in_specs, out_specs=out_specs, check_vma=False)
```

time: 42.6 us -> 38.7 us (0.908)
  Pallas kernels: 41.8 us -> 37.8 us
    pallas_call x1, Pallas kernels: 40.4 us -> 36.3 us  [local(): pl.pallas_call(functools.partial(kernel, tiles_n), out_shape=(pltpu.VMEM(...]
where the time goes in v2:
time: 38.7 us; the launch traced here: 38.6 us
  Pallas kernels  37.8 us (98%)
  between operations  0.8 us (2%)
    pallas_call x1, Pallas kernels, local(): pl.pallas_call(functools.partial(kernel, tiles_n), out_shape=(pltpu.VMEM(...  36.3 us
    pallas_call x1, Pallas kernels, local(): pl.pallas_call(write_out, out_shape=(jax.ShapeDtypeStruct(scores.shape, F...  1.43 us

profile of v2, /device:TPU:0, one launch (start us, length us, event | category | flops | bytes accessed | tf_op | source)
XLA Modules:
  0.0 38.6 jit_solution(6385811441489522336)
XLA Ops:
  0.6 36.3 %shard_map.122 = (f32[2,2,384,384]{3,2,1,0:T(8,128)S(1)}, f32[2,2]{1,0:T(2,128)S(1)}) custom-call(s32[2]{0:T(128)} %owner.1, s32[2,2]{1,0:T(2,128)} %picks.1, s32[1,2]{1,0:T(1,128)} %order.1, f32[8,2,128,128]{3,2,1,0:T(8,128)} %refs_0_.1, f32[2,384,384]{2,1,0:T(8,128)} %refs_1_.1, bf16[256,768]{1,0:T(8,128)(2,1)} %constant.12.clone.refs_2_, ...), custom_call_target="tpu_custom_call" | custom-call | tf_op jit(solution)/shard_map/pallas_call | solution.py:361
  37.0 1.4 %shard_map.123 = (f32[2,2,384,384]{3,2,1,0:T(8,128)}, f32[2,2]{1,0:T(2,128)}) custom-call(f32[2,2,384,384]{3,2,1,0:T(8,128)S(1)} %get-tuple-element.4.scores, f32[2,2]{1,0:T(2,128)S(1)} %get-tuple-element.5.peaks), custom_call_target="tpu_custom_call" | custom-call | tf_op jit(solution)/shard_map/pallas_call | solution.py:381

commit v3 on v2

--- a/solution.py
+++ b/solution.py
@@ -29,6 +29,14 @@
     return np.concatenate([np.cos(angle), np.sin(angle)], axis=0).astype(np.float32)
 
 
+def cyclic_matrix(extent):
+    span = 2 * extent
+    angle = (np.arange(extent)[:, None] * np.arange(span)[None, :] % span) * (2 * math.pi / span)
+    cosine, sine = np.cos(angle), np.sin(angle)
+    sine[0] = 1 - 2 * (np.arange(span) % 2)
+    return np.concatenate([cosine, sine], axis=0).astype(np.float32)
+
+
 def halves(matrix):
     high = matrix.astype(BF16)
     low = (matrix - high.astype(np.float32)).astype(BF16)
@@ -37,26 +45,18 @@
 
 def constants(extent):
     forward = transform_matrix(extent)
+    rings = [cyclic_matrix(extent), forward]
     fh, fl = halves(forward)
     row_left = np.concatenate([fh, fl, fh], axis=1)
-    ft = np.ascontiguousarray(forward.T)
-    th, tl = halves(ft)
-    col_right = np.stack([th, tl])
-    back = forward[:, :extent] * np.float32(1.0 / extent)
-    bh, bl = halves(back)
-    back_right = np.stack([bh, bl])
-    back_left = np.concatenate([bh.T, bl.T, bh.T], axis=1)
+    col_right = np.stack([np.stack(halves(np.ascontiguousarray(r.T))) for r in rings])
+    bh, bl = halves(np.ascontiguousarray(forward[:, :extent].T) * np.float32(1.0 / extent))
+    back_left = np.concatenate([bh, bh, bl], axis=1)
+    back_right = np.stack([np.stack(halves(r * np.float32(0.5 / extent))) for r in rings])
     offset = np.arange(2 * extent)[None, :] - np.arange(extent)[:, None]
     band = ((offset >= 0) & (offset < extent)).astype(BF16)
     band_left = np.concatenate([band, band], axis=1)
     band_right = np.ascontiguousarray(band.T)
     return [jnp.asarray(c) for c in (row_left, col_right, back_left, back_right, band_left, band_right)]
-
-
-def combine(y, e):
-    a, b = y[:e, :e], y[:e, e:]
-    c, d = y[e:, :e], y[e:, e:]
-    return a - d, b + c, a + d, c - b
 
 
 class Transforms:
@@ -67,15 +67,36 @@
         self.nc = self.cols // self.e
         self.entries = self.layers * self.e * self.e
 
-    def rows_of(self, b, window):
+    def special(self):
+        return lax.broadcasted_iota(jnp.int32, (self.e, self.e), 1) == 0
+
+    def combine(self, y, cyclic):
+        e = self.e
+        a, b = y[:e, :e], y[:e, e:]
+        c, d = y[e:, :e], y[e:, e:]
+        parts = a - d, b + c, a + d, c - b
+        if cyclic:
+            first = self.special()
+            parts = [jnp.where(first, own, part) for own, part in zip((a, c, b, d), parts)]
+        return parts
+
+    def weights(self, matrix, ring, rows):
+        return jnp.concatenate([matrix[ring, 0, :rows], matrix[ring, 0, :rows], matrix[ring, 1, :rows]], axis=0)
+
+    def tile_of(self, b, window):
         e, squares = self.e, None
         for l in range(self.layers):
             x = window(l)
             squares = x * x if squares is None else squares + x * x
             xh, xl = split(x)
             y = mm(self.row_left[...], jnp.concatenate([xh, xh, xl], axis=0))
-            h, low = split(y)
-            self.yh[l], self.yl[l] = h, low
+            head, middle, tail = y[:, :e], y[:, e:2 * e], y[:, 2 * e:]
+            mh, ml = split(middle)
+            for ring, start in enumerate((head + tail, head - tail)):
+                sh, sl = split(start)
+                y = mm(jnp.concatenate([sh, mh, sl, ml, sh, mh], axis=1), self.weights(self.col_right, ring, 2 * e))
+                for n, part in enumerate(self.combine(y, ring == 0)):
+                    self.tile_parts[b, l, ring, n] = part
         sh, sl = split(squares)
         energy = mm(self.band_left[...], jnp.concatenate([sh, sl], axis=0))
         eh, el = split(energy)
@@ -85,59 +106,51 @@
             total = mm(eh[:, at], self.band_right[:width]) + mm(el[:, at], self.band_right[:width])
             self.inv[b, :, c * e:(c + 1) * e] = 1.0 / jnp.sqrt(total / self.entries + 1e-05)
 
-    def columns_of(self, b):
-        e = self.e
-        for c in range(self.nc):
-            width = min(2, self.nc - c) * e
-            at = slice(c * e, c * e + width)
+    def clip_of(self, k, layer_at):
+        e, span, row_left = self.e, self.span, self.row_left
+        chosen = [layer_at(l) for l in range(self.layers)]
+        total = sum(x * x for x in chosen)
+        ch, cl = split(jnp.concatenate(chosen, axis=1))
+        left = jnp.concatenate([row_left[:, n * span:n * span + e] for n in range(3)], axis=1)
+        first = mm(left, jnp.concatenate([ch, ch, cl], axis=0))
+        fh, fl = split(jnp.concatenate([first[:, l * e:(l + 1) * e] for l in range(self.layers)], axis=0))
+        left = jnp.concatenate([fh, fl, fh], axis=1)
+        for ring in range(2):
+            y = mm(left, self.weights(self.col_right, ring, e))
             for l in range(self.layers):
-                h, low = self.yh[l, :, at], self.yl[l, :, at]
-                y = mm(h, self.col_right[0, :width]) + mm(low, self.col_right[0, :width]) + mm(h, self.col_right[1, :width])
-                for n, part in enumerate(combine(y, e)):
-                    self.tile_parts[b, c, l, n] = part
-
-    def clip_of(self, k, layer_at):
-        e, span, row_left, col_right = self.e, self.span, self.row_left, self.col_right
-        total = jnp.zeros((e, e), F32)
-        for l in range(self.layers):
-            chosen = layer_at(l)
-            total = total + chosen * chosen
-            ch, cl = split(chosen)
-            first = mm(row_left[:, :e], ch) + mm(row_left[:, span:span + e], ch) + mm(row_left[:, :e], cl)
-            fh, fl = split(first)
-            second = mm(fh, col_right[0, :e]) + mm(fl, col_right[0, :e]) + mm(fh, col_right[1, :e])
-            for n, part in enumerate(combine(second, e)):
-                self.spectra[k, l, n] = part
+                for n, part in enumerate(self.combine(y[l * span:(l + 1) * span], ring == 0)):
+                    self.spectra[k, l, ring, n] = part
         mean = jnp.sum(total, keepdims=True) / self.entries
         return 1.0 / (math.sqrt(self.entries) * jnp.sqrt(mean + 1e-05))
 
     def inverse_of(self, b, k, clip_scale):
-        e = self.e
-        for c in range(self.nc):
+        e, rings = self.e, []
+        for ring in range(2):
             u1 = u2 = v1 = v2 = None
             for l in range(self.layers):
-                p1, p2, q1, q2 = (self.tile_parts[b, c, l, n] for n in range(4))
-                c1, c2, d1, d2 = (self.spectra[k, self.order[0, l], n] for n in range(4))
+                p1, p2, q1, q2 = (self.tile_parts[b, l, ring, n] for n in range(4))
+                c1, c2, d1, d2 = (self.spectra[k, self.order[0, l], ring, n] for n in range(4))
                 t = (p1 * c1 + p2 * c2, p2 * c1 - p1 * c2, q1 * d1 + q2 * d2, q2 * d1 - q1 * d2)
                 if u1 is None:
                     u1, u2, v1, v2 = t
                 else:
                     u1, u2, v1, v2 = u1 + t[0], u2 + t[1], v1 + t[2], v2 + t[3]
-            z = jnp.concatenate([
-                jnp.concatenate([u1 + v1, u2 - v2], axis=1),
-                jnp.concatenate([u2 + v2, v1 - u1], axis=1)], axis=0)
+            parts = u1 + v1, u2 - v2, u2 + v2, v1 - u1
+            if ring == 0:
+                first = self.special()
+                parts = [jnp.where(first, own, part) for own, part in zip((u1, v1, u2, v2), parts)]
+            z = jnp.concatenate([jnp.concatenate(parts[:2], axis=1), jnp.concatenate(parts[2:], axis=1)], axis=0)
             zh, zl = split(z)
-            w = mm(zh, self.back_right[0]) + mm(zl, self.back_right[0]) + mm(zh, self.back_right[1])
-            h, low = split(w)
-            self.wh[k, :, c * e:(c + 1) * e] = h
-            self.wl[k, :, c * e:(c + 1) * e] = low
-        out = mm(self.back_left[...], jnp.concatenate([self.wh[k], self.wh[k], self.wl[k]], axis=0))
-        out = out * self.inv[b] * (clip_scale * 0.5)
-        self.scores[k // self.per_block, k % self.per_block, pl.ds(pl.multiple_of(b * e, e), e)] = out
-        top = jnp.max(out, axis=0, keepdims=True)
+            wh, wl = split(mm(self.back_left[...], jnp.concatenate([zh, zl, zh], axis=0)))
+            rings.append(mm(jnp.concatenate([wh, wl, wh], axis=1), self.weights(self.back_right, ring, 2 * e)))
+        scale = clip_scale * 0.5
         best = self.peaks[k:k + 1]
         for c in range(self.nc):
-            best = jnp.maximum(best, top[:, c * e:(c + 1) * e])
+            n = c % 2
+            even, odd = (r[:, n * e:(n + 1) * e] for r in rings)
+            out = (even + odd if c < 2 else even - odd) * (self.inv[b, :, c * e:(c + 1) * e] * scale)
+            self.scores[k // self.per_block, k % self.per_block, b * e:(b + 1) * e, c * e:(c + 1) * e] = out
+            best = jnp.maximum(best, jnp.max(out, axis=0, keepdims=True))
         self.peaks[k:k + 1] = best
 
 
@@ -150,7 +163,7 @@
 def kernel(tiles_n, owner, picks, order, *refs):
     sources = refs[:8]
     (scores, peak_out,
-           yh, yl, inv, tile_parts, spectra, wh, wl, peaks, slots,
+           inv, tile_parts, spectra, peaks, slots,
            stage, land, full, halo_in,
            rs_send, rs_recv, ag_send, near_recv, far_recv, pair_send, pair_recv,
            halo_send, halo_recv, peak_send, peak_recv,
@@ -167,8 +180,8 @@
     nr = rows // e
     count = picks.shape[0] * per_block
     work = Transforms(dict(row_left=row_left, col_right=col_right, back_left=back_left, back_right=back_right,
-                           band_left=band_left, band_right=band_right, scores=scores, yh=yh, yl=yl, inv=inv,
-                           tile_parts=tile_parts, spectra=spectra, wh=wh, wl=wl, peaks=peaks, order=order),
+                           band_left=band_left, band_right=band_right, scores=scores, inv=inv,
+                           tile_parts=tile_parts, spectra=spectra, peaks=peaks, order=order),
                       (layers, rows, cols, e, per_block, count))
     parity = lax.rem(g, 2)
     other_g = g + 1 - 2 * parity
@@ -235,8 +248,7 @@
     for load in loads[1:]:
         load.wait()
     for b in range(nr - 1):
-        work.rows_of(b, lambda l: tiles[l, b * e:(b + 2) * e])
-        work.columns_of(b)
+        work.tile_of(b, lambda l: tiles[l, b * e:(b + 2) * e])
 
     @pl.when(is_hub)
     def _():
@@ -298,8 +310,7 @@
     @pl.when(t < tiles_n - 1)
     def _():
         halo.wait_recv()
-    work.rows_of(nr - 1, lambda l: jnp.concatenate([tiles[l, rows - e:], halo_in[l]], axis=0))
-    work.columns_of(nr - 1)
+    work.tile_of(nr - 1, lambda l: jnp.concatenate([tiles[l, rows - e:], halo_in[l]], axis=0))
     for k in range(count):
         work.inverse_of(nr - 1, k, scale[k])
 
@@ -346,7 +357,8 @@
 def local(tiles, library, block_owner, block_clips, layer_order):
     layers, rows, cols = tiles.shape
     e = library.shape[-1]
-    span, nr, nc = 2 * e, rows // e, cols // e
+    nr = rows // e
+    assert cols == 3 * e
     blocks, per_block = block_clips.shape
     count = blocks * per_block
     slabs = count * layers
@@ -365,10 +377,8 @@
         in_specs=[smem] * 3 + [pl.BlockSpec(memory_space=pltpu.HBM)] * 8,
         out_specs=(vmem, vmem),
         scratch_shapes=[
-            pltpu.VMEM((layers, span, cols), BF16), pltpu.VMEM((layers, span, cols), BF16),
             pltpu.VMEM((nr, e, cols), F32),
-            pltpu.VMEM((nr, nc, layers, 4, e, e), F32), pltpu.VMEM((count, layers, 4, e, e), F32),
-            pltpu.VMEM((count, span, cols), BF16), pltpu.VMEM((count, span, cols), BF16),
+            pltpu.VMEM((nr, layers, 2, 4, e, e), F32), pltpu.VMEM((count, layers, 2, 4, e, e), F32),
             pltpu.VMEM((lines, e), F32), pltpu.VMEM((tiles_n - 1, lines, e), F32),
             pltpu.VMEM((lanes, e, e), F32), pltpu.VMEM((tiles_n - 1, lanes, e // HUBS, e), F32),
             pltpu.VMEM((2, lanes, e, e), F32), pltpu.VMEM((layers, e, cols), F32),

time: 38.7 us -> 34.7 us (0.90)
  Pallas kernels: 37.8 us -> 33.9 us
    pallas_call x1, Pallas kernels: 36.3 us -> 32.5 us  [local(): pl.pallas_call(functools.partial(kernel, tiles_n), out_shape=(pltpu.VMEM(...]
where the time goes in v3:
time: 34.7 us; the launch traced here: 34.5 us
  Pallas kernels  33.9 us (98%)
  between operations  0.64 us (2%)
    pallas_call x1, Pallas kernels, local(): pl.pallas_call(functools.partial(kernel, tiles_n), out_shape=(pltpu.VMEM(...  32.5 us
    pallas_call x1, Pallas kernels, local(): pl.pallas_call(write_out, out_shape=(jax.ShapeDtypeStruct(scores.shape, F...  1.43 us

profile of v3, /device:TPU:0, one launch (start us, length us, event | category | flops | bytes accessed | tf_op | source)
XLA Modules:
  0.0 34.5 jit_solution(2666187613853523800)
XLA Ops:
  0.6 32.5 %shard_map.122 = (f32[2,2,384,384]{3,2,1,0:T(8,128)S(1)}, f32[2,2]{1,0:T(2,128)S(1)}) custom-call(s32[2]{0:T(128)} %owner.1, s32[2,2]{1,0:T(2,128)} %picks.1, s32[1,2]{1,0:T(1,128)} %order.1, f32[8,2,128,128]{3,2,1,0:T(8,128)} %refs_0_.1, f32[2,384,384]{2,1,0:T(8,128)} %refs_1_.1, bf16[256,768]{1,0:T(8,128)(2,1)} %constant.12.clone.refs_2_, ...), custom_call_target="tpu_custom_call" | custom-call | tf_op jit(solution)/shard_map/pallas_call | solution.py:373
  33.1 1.4 %shard_map.123 = (f32[2,2,384,384]{3,2,1,0:T(8,128)}, f32[2,2]{1,0:T(2,128)}) custom-call(f32[2,2,384,384]{3,2,1,0:T(8,128)S(1)} %get-tuple-element.4.scores, f32[2,2]{1,0:T(2,128)S(1)} %get-tuple-element.5.peaks), custom_call_target="tpu_custom_call" | custom-call | tf_op jit(solution)/shard_map/pallas_call | solution.py:391

commit v4 on v3

--- a/solution.py
+++ b/solution.py
@@ -86,7 +86,7 @@
     def tile_of(self, b, window):
         e, squares = self.e, None
         for l in range(self.layers):
-            x = window(l)
+            x = window(self.layer_of[l])
             squares = x * x if squares is None else squares + x * x
             xh, xl = split(x)
             y = mm(self.row_left[...], jnp.concatenate([xh, xh, xl], axis=0))
@@ -121,49 +121,59 @@
                 for n, part in enumerate(self.combine(y[l * span:(l + 1) * span], ring == 0)):
                     self.spectra[k, l, ring, n] = part
         mean = jnp.sum(total, keepdims=True) / self.entries
-        return 1.0 / (math.sqrt(self.entries) * jnp.sqrt(mean + 1e-05))
-
-    def inverse_of(self, b, k, clip_scale):
+        self.scale[k] = jnp.broadcast_to(0.5 / (math.sqrt(self.entries) * jnp.sqrt(mean + 1e-05)), (1, e))
+
+    def product_of(self, b, k, ring):
+        u1 = u2 = v1 = v2 = None
+        for l in range(self.layers):
+            p1, p2, q1, q2 = (self.tile_parts[b, l, ring, n] for n in range(4))
+            c1, c2, d1, d2 = (self.spectra[k, l, ring, n] for n in range(4))
+            t = (p1 * c1 + p2 * c2, p2 * c1 - p1 * c2, q1 * d1 + q2 * d2, q2 * d1 - q1 * d2)
+            if u1 is None:
+                u1, u2, v1, v2 = t
+            else:
+                u1, u2, v1, v2 = u1 + t[0], u2 + t[1], v1 + t[2], v2 + t[3]
+        parts = u1 + v1, u2 - v2, u2 + v2, v1 - u1
+        if ring == 0:
+            first = self.special()
+            parts = [jnp.where(first, own, part) for own, part in zip((u1, v1, u2, v2), parts)]
+        return jnp.concatenate([jnp.concatenate(parts[:2], axis=1), jnp.concatenate(parts[2:], axis=1)], axis=0)
+
+    def rows_of(self, z):
+        e, span, left = self.e, self.span, self.back_left
+        zh, zl = split(z)
+        both = mm(jnp.concatenate([left[:, :span], left[:, 2 * span:]], axis=0), zh)
+        return both[:e] + both[e:] + mm(left[:, :span], zl)
+
+    def inverse_of(self, items):
         e, rings = self.e, []
         for ring in range(2):
-            u1 = u2 = v1 = v2 = None
-            for l in range(self.layers):
-                p1, p2, q1, q2 = (self.tile_parts[b, l, ring, n] for n in range(4))
-                c1, c2, d1, d2 = (self.spectra[k, self.order[0, l], ring, n] for n in range(4))
-                t = (p1 * c1 + p2 * c2, p2 * c1 - p1 * c2, q1 * d1 + q2 * d2, q2 * d1 - q1 * d2)
-                if u1 is None:
-                    u1, u2, v1, v2 = t
-                else:
-                    u1, u2, v1, v2 = u1 + t[0], u2 + t[1], v1 + t[2], v2 + t[3]
-            parts = u1 + v1, u2 - v2, u2 + v2, v1 - u1
-            if ring == 0:
-                first = self.special()
-                parts = [jnp.where(first, own, part) for own, part in zip((u1, v1, u2, v2), parts)]
-            z = jnp.concatenate([jnp.concatenate(parts[:2], axis=1), jnp.concatenate(parts[2:], axis=1)], axis=0)
-            zh, zl = split(z)
-            wh, wl = split(mm(self.back_left[...], jnp.concatenate([zh, zl, zh], axis=0)))
-            rings.append(mm(jnp.concatenate([wh, wl, wh], axis=1), self.weights(self.back_right, ring, 2 * e)))
-        scale = clip_scale * 0.5
-        best = self.peaks[k:k + 1]
-        for c in range(self.nc):
-            n = c % 2
-            even, odd = (r[:, n * e:(n + 1) * e] for r in rings)
-            out = (even + odd if c < 2 else even - odd) * (self.inv[b, :, c * e:(c + 1) * e] * scale)
-            self.scores[k // self.per_block, k % self.per_block, b * e:(b + 1) * e, c * e:(c + 1) * e] = out
-            best = jnp.maximum(best, jnp.max(out, axis=0, keepdims=True))
-        self.peaks[k:k + 1] = best
+            wh, wl = zip(*(split(self.rows_of(self.product_of(b, k, ring))) for b, k in items))
+            wh, wl = jnp.concatenate(wh, axis=0), jnp.concatenate(wl, axis=0)
+            both = mm(jnp.concatenate([wh, wl], axis=0), self.back_right[ring, 0])
+            rings.append(both[:len(items) * e] + both[len(items) * e:] + mm(wh, self.back_right[ring, 1]))
+        for n, (b, k) in enumerate(items):
+            scale = self.scale[k]
+            best = self.peaks[k]
+            for c in range(self.nc):
+                even, odd = (r[n * e:(n + 1) * e, c % 2 * e:(c % 2 + 1) * e] for r in rings)
+                out = (even + odd if c < 2 else even - odd) * (self.inv[b, :, c * e:(c + 1) * e] * scale)
+                at = pl.ds(pl.multiple_of(b * e, e), e)
+                self.scores[k // self.per_block, lax.rem(k, self.per_block), at, c * e:(c + 1) * e] = out
+                best = jnp.maximum(best, jnp.max(out, axis=0, keepdims=True))
+            self.peaks[k] = best
 
 
 MESH = pl.DeviceIdType.MESH
 PLANE = 4
 HUBS = 2 * PLANE
-CHUNKS = 4
+UNROLL = 4
 
 
 def kernel(tiles_n, owner, picks, order, *refs):
     sources = refs[:8]
     (scores, peak_out,
-           inv, tile_parts, spectra, peaks, slots,
+           inv, tile_parts, spectra, scale, peaks, best, slots,
            stage, land, full, halo_in,
            rs_send, rs_recv, ag_send, near_recv, far_recv, pair_send, pair_recv,
            halo_send, halo_recv, peak_send, peak_recv,
@@ -179,9 +189,10 @@
     e = library.shape[-1]
     nr = rows // e
     count = picks.shape[0] * per_block
+    layer_of = [sum(jnp.where(order[0, l] == own, l, 0) for l in range(1, layers)) for own in range(layers)]
     work = Transforms(dict(row_left=row_left, col_right=col_right, back_left=back_left, back_right=back_right,
                            band_left=band_left, band_right=band_right, scores=scores, inv=inv,
-                           tile_parts=tile_parts, spectra=spectra, peaks=peaks, order=order),
+                           tile_parts=tile_parts, spectra=spectra, scale=scale, peaks=best, layer_of=layer_of),
                       (layers, rows, cols, e, per_block, count))
     parity = lax.rem(g, 2)
     other_g = g + 1 - 2 * parity
@@ -205,7 +216,7 @@
         greet((other_g, first_hub + 2 * n + core))
 
     lanes = count * layers // 2
-    width = lanes // CHUNKS
+    width = lanes // count
     part = e // HUBS
     loads[0].wait()
     for j in range(lanes):
@@ -229,7 +240,7 @@
         return pl.ds(m * width, width)
 
     mine = pl.ds(pl.multiple_of(core * (e // 2), e // 2), e // 2)
-    for m in range(CHUNKS):
+    for m in range(count):
         for n in range(HUBS):
             hub = lax.rem(t + n, HUBS)
             target = first_hub + hub
@@ -245,15 +256,19 @@
         halo_in[...] = jnp.zeros_like(halo_in)
 
     peaks[...] = jnp.full(peaks.shape, -jnp.inf, F32)
+    best[...] = jnp.full(best.shape, -jnp.inf, F32)
     for load in loads[1:]:
         load.wait()
-    for b in range(nr - 1):
-        work.tile_of(b, lambda l: tiles[l, b * e:(b + 2) * e])
+    def tile_block(b, carry):
+        work.tile_of(b, lambda l: tiles[l, pl.ds(pl.multiple_of(b * e, e), 2 * e)])
+        return carry
+
+    lax.fori_loop(0, nr - 1, tile_block, 0)
 
     @pl.when(is_hub)
     def _():
         at = place(t - first_hub)
-        for m in range(CHUNKS):
+        for m in range(count):
             remote(land.at[:, lane(m)], land.at[:, lane(m)], rs_send.at[m], rs_recv.at[m], partner).wait_recv()
             total = stage[lane(m), at]
             for d in range(tiles_n - 1):
@@ -266,8 +281,8 @@
                 remote(piece, piece, ag_send.at[m], far_recv.at[m], (other_g, lax.rem(t + 2 * n, tiles_n))).start()
 
     halo = remote(tiles.at[:, pl.ds(0, e)], halo_in, halo_send, halo_recv, (g, t - 1))
-    pairs = [remote(full.at[:, lane(m), mine], full.at[:, lane(m), mine], pair_send.at[m], pair_recv.at[m], partner)
-             for m in range(CHUNKS)]
+    def pair(m):
+        return remote(full.at[:, lane(m), mine], full.at[:, lane(m), mine], pair_send.at[m], pair_recv.at[m], partner)
 
     def arrive(m):
         far = full.at[0, lane(m), mine]
@@ -282,43 +297,46 @@
         def _():
             remote(far, far, ag_send.at[m], near_recv.at[m], partner).wait_recv()
 
-        pairs[m].start()
-
-    scale = {}
-
-    def clips_in(m):
-        slabs = range(2 * m * width, 2 * (m + 1) * width)
-        return [k for k in range(count) if (k + 1) * layers - 1 in slabs]
-
-    def slab_of(k, l):
-        return full[(k * layers + l) % 2, (k * layers + l) // 2]
-
-    for m in range(CHUNKS + 1):
-        if m < CHUNKS:
-            arrive(m)
-        if m == 0:
-            @pl.when(t > 0)
-            def _():
-                halo.start()
-        else:
-            pairs[m - 1].wait_recv()
-            for k in clips_in(m - 1):
-                scale[k] = work.clip_of(k, lambda l: slab_of(k, l))
-                for b in range(nr - 1):
-                    work.inverse_of(b, k, scale[k])
+        pair(m).start()
+
+    arrive(0)
+
+    @pl.when(t > 0)
+    def _():
+        halo.start()
+
+    def clip_block(k, carry):
+        @pl.when(k < count - 1)
+        def _():
+            arrive(k + 1)
+
+        pair(k).wait_recv()
+        work.clip_of(k, lambda l: full[l, k])
+        for b in range(nr - 1):
+            work.inverse_of([(b, k)])
+        return carry
+
+    lax.fori_loop(0, count, clip_block, 0)
 
     @pl.when(t < tiles_n - 1)
     def _():
         halo.wait_recv()
     work.tile_of(nr - 1, lambda l: jnp.concatenate([tiles[l, rows - e:], halo_in[l]], axis=0))
+
+    def last_block(k, carry):
+        for n in range(UNROLL):
+            work.inverse_of([(nr - 1, UNROLL * k + n)])
+        return carry
+
+    lax.fori_loop(0, count // UNROLL, last_block, 0)
     for k in range(count):
-        work.inverse_of(nr - 1, k, scale[k])
+        peaks[k:k + 1] = best[k]
 
     copies = [remote(peaks, slots.at[n], peak_send, peak_recv, target) for n, target in enumerate(others)]
     for copy in copies:
         copy.start()
-    for m in range(CHUNKS):
-        pairs[m].wait_send()
+    for m in range(count):
+        pair(m).wait_send()
 
         @pl.when(is_hub)
         def _(m=m):
@@ -335,14 +353,14 @@
     def _():
         halo.wait_send()
 
-    best = peaks[...]
+    top = peaks[...]
     remote(slots, slots, peak_send, peak_recv, partner).wait_recv()
     for n in range(tiles_n - 1):
-        best = jnp.maximum(best, slots[n])
-    best = jnp.max(best, axis=1, keepdims=True)
+        top = jnp.maximum(top, slots[n])
+    top = jnp.max(top, axis=1, keepdims=True)
     for k in range(count):
         at = k % per_block
-        peak_out[k // per_block:k // per_block + 1, at:at + 1] = best[k:k + 1]
+        peak_out[k // per_block:k // per_block + 1, at:at + 1] = top[k:k + 1]
     remote(slots, slots, peak_send, peak_recv, partner).wait_send()
 
 
@@ -363,7 +381,7 @@
     count = blocks * per_block
     slabs = count * layers
     lanes = slabs // 2
-    assert slabs % 2 == 0 and lanes % CHUNKS == 0
+    assert layers == 2 and count % UNROLL == 0
     tiles_n = lax.axis_size("tile")
     smem = pl.BlockSpec(memory_space=pltpu.SMEM)
     vmem = pl.BlockSpec(memory_space=pltpu.VMEM)
@@ -379,10 +397,11 @@
         scratch_shapes=[
             pltpu.VMEM((nr, e, cols), F32),
             pltpu.VMEM((nr, layers, 2, 4, e, e), F32), pltpu.VMEM((count, layers, 2, 4, e, e), F32),
-            pltpu.VMEM((lines, e), F32), pltpu.VMEM((tiles_n - 1, lines, e), F32),
+            pltpu.VMEM((count, 1, e), F32), pltpu.VMEM((lines, e), F32), pltpu.VMEM((count, 1, e), F32),
+            pltpu.VMEM((tiles_n - 1, lines, e), F32),
             pltpu.VMEM((lanes, e, e), F32), pltpu.VMEM((tiles_n - 1, lanes, e // HUBS, e), F32),
             pltpu.VMEM((2, lanes, e, e), F32), pltpu.VMEM((layers, e, cols), F32),
-            *[dma((CHUNKS,))] * 7, dma, dma, dma, dma,
+            *[dma((count,))] * 7, dma, dma, dma, dma,
         ] + [pltpu.VMEM(a.shape, a.dtype) for a in operands] + [dma((len(operands),))],
         compiler_params=pltpu.CompilerParams(collective_id=0, has_side_effects=True, vmem_limit_bytes=64600000),
     )(block_owner, block_clips, layer_order, *operands)

time: 34.7 us -> 33.9 us (0.977)
  Pallas kernels: 33.9 us -> 33.1 us
    pallas_call x1, Pallas kernels: 32.5 us -> 31.7 us  [local(): pl.pallas_call(functools.partial(kernel, tiles_n), out_shape=(pltpu.VMEM(...]
where the time goes in v4:
time: 33.9 us; the launch traced here: 33.8 us
  Pallas kernels  33.1 us (98%)
  between operations  0.64 us (2%)
    pallas_call x1, Pallas kernels, local(): pl.pallas_call(functools.partial(kernel, tiles_n), out_shape=(pltpu.VMEM(...  31.7 us
    pallas_call x1, Pallas kernels, local(): pl.pallas_call(write_out, out_shape=(jax.ShapeDtypeStruct(scores.shape, F...  1.43 us

profile of v4, /device:TPU:0, one launch (start us, length us, event | category | flops | bytes accessed | tf_op | source)
XLA Modules:
  0.0 33.8 jit_solution(6842780454124496536)
XLA Ops:
  0.6 31.7 %shard_map.122 = (f32[2,2,384,384]{3,2,1,0:T(8,128)S(1)}, f32[2,2]{1,0:T(2,128)S(1)}) custom-call(s32[2]{0:T(128)} %owner.1, s32[2,2]{1,0:T(2,128)} %picks.1, s32[1,2]{1,0:T(1,128)} %order.1, f32[8,2,128,128]{3,2,1,0:T(8,128)} %refs_0_.1, f32[2,384,384]{2,1,0:T(8,128)} %refs_1_.1, bf16[256,768]{1,0:T(8,128)(2,1)} %constant.12.clone.refs_2_, ...), custom_call_target="tpu_custom_call" | custom-call | tf_op jit(solution)/shard_map/pallas_call | solution.py:391
  32.3 1.4 %shard_map.123 = (f32[2,2,384,384]{3,2,1,0:T(8,128)}, f32[2,2]{1,0:T(2,128)}) custom-call(f32[2,2,384,384]{3,2,1,0:T(8,128)S(1)} %get-tuple-element.4.scores, f32[2,2]{1,0:T(2,128)S(1)} %get-tuple-element.5.peaks), custom_call_target="tpu_custom_call" | custom-call | tf_op jit(solution)/shard_map/pallas_call | solution.py:410

commit v5 on v4

--- a/solution.py
+++ b/solution.py
@@ -159,7 +159,7 @@
                 even, odd = (r[n * e:(n + 1) * e, c % 2 * e:(c % 2 + 1) * e] for r in rings)
                 out = (even + odd if c < 2 else even - odd) * (self.inv[b, :, c * e:(c + 1) * e] * scale)
                 at = pl.ds(pl.multiple_of(b * e, e), e)
-                self.scores[k // self.per_block, lax.rem(k, self.per_block), at, c * e:(c + 1) * e] = out
+                self.scores[k // self.per_block, k % self.per_block, at, c * e:(c + 1) * e] = out
                 best = jnp.maximum(best, jnp.max(out, axis=0, keepdims=True))
             self.peaks[k] = best
 
@@ -305,30 +305,22 @@
     def _():
         halo.start()
 
-    def clip_block(k, carry):
-        @pl.when(k < count - 1)
-        def _():
+    for k in range(count):
+        if k < count - 1:
             arrive(k + 1)
-
         pair(k).wait_recv()
+        for b in range(nr - 1 if k else 0):
+            work.inverse_of([(b, k - 1)])
         work.clip_of(k, lambda l: full[l, k])
-        for b in range(nr - 1):
-            work.inverse_of([(b, k)])
-        return carry
-
-    lax.fori_loop(0, count, clip_block, 0)
 
     @pl.when(t < tiles_n - 1)
     def _():
         halo.wait_recv()
     work.tile_of(nr - 1, lambda l: jnp.concatenate([tiles[l, rows - e:], halo_in[l]], axis=0))
-
-    def last_block(k, carry):
-        for n in range(UNROLL):
-            work.inverse_of([(nr - 1, UNROLL * k + n)])
-        return carry
-
-    lax.fori_loop(0, count // UNROLL, last_block, 0)
+    for b in range(nr - 1):
+        work.inverse_of([(b, count - 1)])
+    for k in range(count):
+        work.inverse_of([(nr - 1, k)])
     for k in range(count):
         peaks[k:k + 1] = best[k]
 

time: 33.9 us -> 33.5 us (0.988)
  Pallas kernels: 33.1 us -> 32.7 us
    pallas_call x1, Pallas kernels: 31.7 us -> 31.3 us  [local(): pl.pallas_call(functools.partial(kernel, tiles_n), out_shape=(pltpu.VMEM(...]
where the time goes in v5:
time: 33.5 us; the launch traced here: 33.4 us
  Pallas kernels  32.7 us (98%)
  between operations  0.64 us (2%)
    pallas_call x1, Pallas kernels, local(): pl.pallas_call(functools.partial(kernel, tiles_n), out_shape=(pltpu.VMEM(...  31.3 us
    pallas_call x1, Pallas kernels, local(): pl.pallas_call(write_out, out_shape=(jax.ShapeDtypeStruct(scores.shape, F...  1.43 us

profile of v5, /device:TPU:0, one launch (start us, length us, event | category | flops | bytes accessed | tf_op | source)
XLA Modules:
  0.0 33.4 jit_solution(13662867860717150030)
XLA Ops:
  0.6 31.3 %shard_map.122 = (f32[2,2,384,384]{3,2,1,0:T(8,128)S(1)}, f32[2,2]{1,0:T(2,128)S(1)}) custom-call(s32[2]{0:T(128)} %owner.1, s32[2,2]{1,0:T(2,128)} %picks.1, s32[1,2]{1,0:T(1,128)} %order.1, f32[8,2,128,128]{3,2,1,0:T(8,128)} %refs_0_.1, f32[2,384,384]{2,1,0:T(8,128)} %refs_1_.1, bf16[256,768]{1,0:T(8,128)(2,1)} %constant.12.clone.refs_2_, ...), custom_call_target="tpu_custom_call" | custom-call | tf_op jit(solution)/shard_map/pallas_call | solution.py:383
  31.9 1.4 %shard_map.123 = (f32[2,2,384,384]{3,2,1,0:T(8,128)}, f32[2,2]{1,0:T(2,128)}) custom-call(f32[2,2,384,384]{3,2,1,0:T(8,128)S(1)} %get-tuple-element.4.scores, f32[2,2]{1,0:T(2,128)S(1)} %get-tuple-element.5.peaks), custom_call_target="tpu_custom_call" | custom-call | tf_op jit(solution)/shard_map/pallas_call | solution.py:402

commit v6 on v5

--- a/solution.py
+++ b/solution.py
@@ -324,9 +324,13 @@
     for k in range(count):
         peaks[k:k + 1] = best[k]
 
-    copies = [remote(peaks, slots.at[n], peak_send, peak_recv, target) for n, target in enumerate(others)]
-    for copy in copies:
-        copy.start()
+    for n in range(tiles_n):
+        target = jnp.where(t < tiles_n // 2, tiles_n - 1 - n, n)
+
+        @pl.when(target != t)
+        def _(target=target):
+            slot = lax.rem(t - target + tiles_n, tiles_n) - 1
+            remote(peaks, slots.at[slot], peak_send, peak_recv, (g, target)).start()
     for m in range(count):
         pair(m).wait_send()
 

time: 33.5 us -> 33.8 us (level)
  no operation moved by 1% of the time
where the time goes in v6:
time: 33.8 us; the launch traced here: 33.6 us
  Pallas kernels  33 us (98%)
  between operations  0.64 us (2%)
    pallas_call x1, Pallas kernels, local(): pl.pallas_call(functools.partial(kernel, tiles_n), out_shape=(pltpu.VMEM(...  31.5 us
    pallas_call x1, Pallas kernels, local(): pl.pallas_call(write_out, out_shape=(jax.ShapeDtypeStruct(scores.shape, F...  1.43 us

profile of v6, /device:TPU:0, one launch (start us, length us, event | category | flops | bytes accessed | tf_op | source)
XLA Modules:
  0.0 33.6 jit_solution(4923094960851884050)
XLA Ops:
  0.6 31.5 %shard_map.122 = (f32[2,2,384,384]{3,2,1,0:T(8,128)S(1)}, f32[2,2]{1,0:T(2,128)S(1)}) custom-call(s32[2]{0:T(128)} %owner.1, s32[2,2]{1,0:T(2,128)} %picks.1, s32[1,2]{1,0:T(1,128)} %order.1, f32[8,2,128,128]{3,2,1,0:T(8,128)} %refs_0_.1, f32[2,384,384]{2,1,0:T(8,128)} %refs_1_.1, bf16[256,768]{1,0:T(8,128)(2,1)} %constant.12.clone.refs_2_, ...), custom_call_target="tpu_custom_call" | custom-call | tf_op jit(solution)/shard_map/pallas_call | solution.py:387
  32.2 1.4 %shard_map.123 = (f32[2,2,384,384]{3,2,1,0:T(8,128)}, f32[2,2]{1,0:T(2,128)}) custom-call(f32[2,2,384,384]{3,2,1,0:T(8,128)S(1)} %get-tuple-element.4.scores, f32[2,2]{1,0:T(2,128)S(1)} %get-tuple-element.5.peaks), custom_call_target="tpu_custom_call" | custom-call | tf_op jit(solution)/shard_map/pallas_call | solution.py:406

commit v7 on v5

--- a/solution.py
+++ b/solution.py
@@ -140,10 +140,9 @@
         return jnp.concatenate([jnp.concatenate(parts[:2], axis=1), jnp.concatenate(parts[2:], axis=1)], axis=0)
 
     def rows_of(self, z):
-        e, span, left = self.e, self.span, self.back_left
+        left = self.back_left
         zh, zl = split(z)
-        both = mm(jnp.concatenate([left[:, :span], left[:, 2 * span:]], axis=0), zh)
-        return both[:e] + both[e:] + mm(left[:, :span], zl)
+        return mm(left[...], jnp.concatenate([zh, zl, zh], axis=0))
 
     def inverse_of(self, items):
         e, rings = self.e, []

time: 33.5 us -> 33.9 us (1.012)
  Pallas kernels: 32.7 us -> 33.1 us
    pallas_call x1, Pallas kernels: 31.3 us -> 31.7 us  [local(): pl.pallas_call(functools.partial(kernel, tiles_n), out_shape=(pltpu.VMEM(...]
where the time goes in v7:
time: 33.9 us; the launch traced here: 33.7 us
  Pallas kernels  33.1 us (98%)
  between operations  0.64 us (2%)
    pallas_call x1, Pallas kernels, local(): pl.pallas_call(functools.partial(kernel, tiles_n), out_shape=(pltpu.VMEM(...  31.7 us
    pallas_call x1, Pallas kernels, local(): pl.pallas_call(write_out, out_shape=(jax.ShapeDtypeStruct(scores.shape, F...  1.43 us

profile of v7, /device:TPU:0, one launch (start us, length us, event | category | flops | bytes accessed | tf_op | source)
XLA Modules:
  0.0 33.7 jit_solution(9146847983983986288)
XLA Ops:
  0.6 31.7 %shard_map.122 = (f32[2,2,384,384]{3,2,1,0:T(8,128)S(1)}, f32[2,2]{1,0:T(2,128)S(1)}) custom-call(s32[2]{0:T(128)} %owner.1, s32[2,2]{1,0:T(2,128)} %picks.1, s32[1,2]{1,0:T(1,128)} %order.1, f32[8,2,128,128]{3,2,1,0:T(8,128)} %refs_0_.1, f32[2,384,384]{2,1,0:T(8,128)} %refs_1_.1, bf16[256,768]{1,0:T(8,128)(2,1)} %constant.12.clone.refs_2_, ...), custom_call_target="tpu_custom_call" | custom-call | tf_op jit(solution)/shard_map/pallas_call | solution.py:382
  32.3 1.4 %shard_map.123 = (f32[2,2,384,384]{3,2,1,0:T(8,128)}, f32[2,2]{1,0:T(2,128)}) custom-call(f32[2,2,384,384]{3,2,1,0:T(8,128)S(1)} %get-tuple-element.4.scores, f32[2,2]{1,0:T(2,128)S(1)} %get-tuple-element.5.peaks), custom_call_target="tpu_custom_call" | custom-call | tf_op jit(solution)/shard_map/pallas_call | solution.py:401
